TPU v7x, 256 devices: a whole 4x4x8 slice. The times are simulated.
256 devices in a mesh: ka: 32 (over z_hi, y, core), pa: 8 (over z_lo, x).
Axes of the slice: x: 4, y: 4, z: 8 (z_hi: 4, z_lo: 2; z = z_hi * 2 + z_lo), core: 2. Of those that a mesh axis runs over, the one named last changes fastest.
Arguments:
- orbitals: bfloat16 [32, 4096, 128], P('ka', 'pa'), may hold values from -0.75 to 0.75
- occupied: int32 [32], P('ka'), may hold values from 32 to 64
- plus_partner: int32 [32], P('ka'), may hold values from 0 to 31, as said below
- minus_partner: int32 [32], P('ka'), may hold values from 0 to 31, as said below
- coulomb: bfloat16 [2, 4096, 4096], P(None, 'pa'), as said below
Outputs:
- exchange_out: float32 [32, 4096, 128], P('ka', 'pa')
Inputs may be any that keep to these rules, and one draw needn't show every extreme that they name: `plus_partner`: a permutation of the 32 window positions. `minus_partner`: the inverse permutation of plus_partner. `coulomb`: each of the two kernels is a symmetric matrix.
All inputs are finite; a program needn't handle non-finite values.
Results may differ from a plain program's by a relative error of at most 0.0003.
Values may be sent and summed in bfloat16 or wider, within the bound.
A program may use at most 128 MiB of HBM per device.

v0:
```python
import jax
import jax.numpy as jnp
from jax import lax
from jax.sharding import PartitionSpec as P

column_block = 1024
pair_dims = (((2,), (2,)), ((0,), (0,)))


def rotate(block):
    bands = block.shape[-1] // 2
    return jnp.concatenate([block[..., bands:], -block[..., :bands]], axis=-1)


def counter_rotate(block):
    bands = block.shape[-1] // 2
    return jnp.concatenate([-block[..., bands:], block[..., :bands]], axis=-1)


def kernel_halves(own_block):
    upper_half = own_block.astype(jnp.float32)
    return (upper_half, counter_rotate(upper_half))


def body(orbitals, occupied, plus_partner, minus_partner, coulomb):
    k_local, points, channels = orbitals.shape
    bands = channels // 2
    band_index = lax.broadcasted_iota(jnp.int32, (1, 1, channels), 2) % bands
    keep_mask = band_index < occupied[:, None, None]
    masked = jnp.where(keep_mask, orbitals, jnp.zeros_like(orbitals))
    gathered = lax.all_gather(masked, "ka", axis=0, tiled=True)
    wanted = jnp.concatenate([plus_partner, minus_partner])
    chosen = jnp.take(gathered, wanted, axis=0).reshape(2, k_local, points, channels)
    partner_turned = rotate(chosen)
    stacked = jnp.concatenate([chosen, orbitals[None]], axis=0)
    initial = jnp.zeros((k_local, points, channels), jnp.float32)
    shard_part = lax.all_gather(stacked, "pa", axis=2, tiled=True)
    amount = shard_part.shape[2]
    stride = min(amount, column_block)
    summed = initial[0]
    for offset in range(0, amount, stride):
        length = min(stride, amount - offset)
        col_block = shard_part[:, 0, offset : offset + length]
        kernel_tile = lax.dynamic_slice_in_dim(coulomb, offset, length, 2).astype(jnp.float32)
        real_part = lax.dot_general(
            chosen[:, 0], col_block[:2], pair_dims, preferred_element_type=jnp.float32
        )
        imag_part = lax.dot_general(
            partner_turned[:, 0], col_block[:2], pair_dims, preferred_element_type=jnp.float32
        )
        mixed_real = kernel_tile[0] * real_part[0] + kernel_tile[1] * real_part[1]
        mixed_imag = kernel_tile[0] * imag_part[0] + kernel_tile[1] * imag_part[1]
        upper_half, lower_half = kernel_halves(col_block[2])
        applied = jnp.dot(
            mixed_real,
            upper_half,
            precision=lax.Precision.HIGHEST,
            preferred_element_type=jnp.float32,
        )
        applied = applied + jnp.dot(
            mixed_imag,
            lower_half,
            precision=lax.Precision.HIGHEST,
            preferred_element_type=jnp.float32,
        )
        summed = summed - applied
    results = [summed]
    return jnp.stack(results)


def solution(mesh):
    placed = (P("ka", "pa", None), P("ka"), P("ka"), P("ka"), P(None, "pa", None))
    return jax.shard_map(
        body, mesh=mesh, in_specs=placed, out_specs=P("ka", "pa", None), check_vma=False
    )
```

profile of v0, /device:TPU:8, one launch (start us, length us, event | category | flops | bytes accessed | tf_op | source)
XLA Modules:
  0.0 159.0 jit_solution(12818980166392069198)
XLA Ops:
  7.2 1.6 broadcast_select_fusion.1
  10.3 62.5 %all-gather.3.cloned.1.call-done = bf16[32,512,128]{2,1,0:T(8,128)(2,1)} async-done(((bf16[1,512,128]{2,1,0:T(8,128)(2,1)}), bf16[32,512,128]{2,1,0:T(8,128)(2,1)}) %all-gather.3.cloned.1.call-update) | async-done | bytes 4194320 | tf_op jit(solution)/shard_map/all_gather | solution.py:31
  72.8 2.8 %gather_fusion = bf16[2,512,128]{2,1,0:T(8,128)(2,1)S(1)} fusion(bf16[32,512,128]{2,1,0:T(8,128)(2,1)} %all-gather.3.cloned.1.call-done, s32[1024]{0:T(1024)S(1)} %pad_clamp_fusion), kind=kCustom, calls=%fused_computation | custom fusion | bytes 524296 | tf_op jit(solution)/shard_map/jit(_take)/gather | solution.py:33
  75.7 1.7 %pad_maximum_fusion = bf16[3,1,512,128]{3,2,0,1:T(8,128)(2,1)} fusion(bf16[1,1,512,128]{3,2,0,1:T(8,128)(2,1)} %bitcast.97, bf16[2,1,512,128]{3,2,0,1:T(8,128)(2,1)S(1)} %bitcast_select_fusion), kind=kLoop, calls=%fused_computation.98 | loop fusion | flops 196608 | bytes 786432 | tf_op jit(solution)/shard_map/concatenate | solution.py:35
  77.4 10.2 %slice_convert_fusion.1 = (f32[2,512,1024]{2,1,0:T(8,128)}, f32[2,512,1024]{2,1,0:T(8,128)}, f32[2,512,1024]{2,1,0:T(8,128)}, f32[2,512,1024]{2,1,0:T(8,128)}) fusion(bf16[2,512,4096]{2,1,0:T(8,128)(2,1)} %param.9), kind=kLoop, calls=%fused_computation.42 | loop fusion | flops 4194304 | bytes 25165824 | tf_op jit(solution)/shard_map/convert_element_type | solution.py:44
  87.9 34.7 %all-gather.5.cloned.1.call-done = bf16[3,1,4096,128]{3,2,0,1:T(8,128)(2,1)} async-done(((bf16[3,1,512,128]{3,2,0,1:T(8,128)(2,1)}), bf16[3,1,4096,128]{3,2,0,1:T(8,128)(2,1)}) %all-gather.5.cloned.1.call-update) | async-done | bytes 3145744 | tf_op jit(solution)/shard_map/all_gather | solution.py:37
  122.5 1.3 fusion.97
  124.6 1.5 copy-done.4
  126.8 1.5 copy-done.3
  128.3 2.0 %fusion.18 = f32[512,128]{1,0:T(8,128)S(1)} fusion(f32[2,512,1024]{2,1,0:T(8,128)S(1)} %fusion.89, f32[2,512,1024]{2,1,0:T(8,128)S(1)} %copy-done.3, f32[1024,64]{1,0:T(8,128)S(1)} %get-tuple-element.18, f32[1024,64]{1,0:T(8,128)S(1)} %get-tuple-element.17), kind=kOutput, calls=%fused_computation.24 | convolution fusion | flops 807010304 | bytes 9175040 | tf_op jit(solution)/shard_map/dot_general | solution.py:60
  131.0 1.5 copy-done.1
  132.5 2.0 %fusion.26 = f32[512,128]{1,0:T(8,128)S(1)} fusion(f32[2,512,1024]{2,1,0:T(8,128)S(1)} %fusion.87, f32[2,512,1024]{2,1,0:T(8,128)S(1)} %copy-done.1, f32[1024,64]{1,0:T(8,128)S(1)} %get-tuple-element.25, f32[1024,64]{1,0:T(8,128)S(1)} %get-tuple-element.26), kind=kOutput, calls=%fused_computation.34 | convolution fusion | flops 807010304 | bytes 9175040 | tf_op jit(solution)/shard_map/dot_general | solution.py:60
  135.2 1.5 copy-done
  136.7 2.0 %fusion.10 = f32[512,128]{1,0:T(8,128)S(1)} fusion(f32[2,512,1024]{2,1,0:T(8,128)S(1)} %fusion.91, f32[2,512,1024]{2,1,0:T(8,128)S(1)} %copy-done, f32[1024,64]{1,0:T(8,128)S(1)} %get-tuple-element.23, f32[1024,64]{1,0:T(8,128)S(1)} %get-tuple-element.24), kind=kOutput, calls=%fused_computation.14 | convolution fusion | flops 807010304 | bytes 9175040 | tf_op jit(solution)/shard_map/dot_general | solution.py:60
  139.4 1.5 copy-done.2
  140.9 2.2 %fusion.2 = f32[512,128]{1,0:T(8,128)S(1)} fusion(f32[2,512,1024]{2,1,0:T(8,128)S(1)} %fusion.93, f32[2,512,1024]{2,1,0:T(8,128)S(1)} %copy-done.2, f32[1024,64]{1,0:T(8,128)S(1)} %get-tuple-element.20, f32[1024,64]{1,0:T(8,128)S(1)} %get-tuple-element.19), kind=kOutput, calls=%fused_computation.4 | convolution fusion | flops 807010304 | bytes 9175040 | tf_op jit(solution)/shard_map/dot_general | solution.py:60
  143.1 0.7 fusion.90
  143.9 0.7 fusion.88
  144.6 0.7 fusion.94
  145.4 0.7 fusion.92
  146.1 1.3 fusion.57
  147.4 1.3 fusion.72
  148.8 1.3 fusion.54
  150.1 2.0 %fusion.69 = f32[1,512,128]{2,1,0:T(8,128)} fusion(f32[512,128]{1,0:T(8,128)S(1)} %fusion.72, f32[512,128]{1,0:T(8,128)S(1)} %fusion.54, f32[512,128]{1,0:T(8,128)S(1)} %fusion.10, f32[2,512,1024]{2,1,0:T(8,128)S(1)} %fusion.92, f32[2,512,1024]{2,1,0:T(8,128)S(1)} %copy-done, bf16[3,1,4096,128]{3,2,0,1:T(8,128)(2,1)S(1)} %copy-done.4), kind=kOutput, calls=%fused_computation.68 | convolution fusion | flops 807075840 | bytes 9699328 | tf_op jit(solution)/shard_map/dot_general | solution.py:54
  (22 shorter events, 4.2 us)
Async XLA Ops:
  6.5 66.3 %all-gather.3.cloned.1.call-start = ((), (), s32[]{:S(2)}) async-start(), calls=%async_computation | async-start | bytes 4325376 | tf_op jit(solution)/shard_map/all_gather | solution.py:31
  8.8 113.7 %all-gather.5.cloned.1.call-start = ((), (), s32[]{:S(2)}) async-start(), calls=%async_computation.1 | async-start | bytes 3538944 | tf_op jit(solution)/shard_map/all_gather | solution.py:37
  124.2 1.9 %copy-start.4 = (bf16[3,1,4096,128]{3,2,0,1:T(8,128)(2,1)S(1)}, bf16[3,1,4096,128]{3,2,0,1:T(8,128)(2,1)}, u32[]{:S(2)}) copy-start(bf16[3,1,4096,128]{3,2,0,1:T(8,128)(2,1)} %all-gather.5.cloned.1.call-done) | copy-start | bytes 9437188
  126.1 2.2 %copy-start.3 = (f32[2,512,1024]{2,1,0:T(8,128)S(1)}, f32[2,512,1024]{2,1,0:T(8,128)}, u32[]{:S(2)}) copy-start(f32[2,512,1024]{2,1,0:T(8,128)} %get-tuple-element.6) | copy-start | bytes 12582916
  130.3 2.2 %copy-start.1 = (f32[2,512,1024]{2,1,0:T(8,128)S(1)}, f32[2,512,1024]{2,1,0:T(8,128)}, u32[]{:S(2)}) copy-start(f32[2,512,1024]{2,1,0:T(8,128)} %get-tuple-element.7) | copy-start | bytes 12582916
  134.5 2.2 %copy-start = (f32[2,512,1024]{2,1,0:T(8,128)S(1)}, f32[2,512,1024]{2,1,0:T(8,128)}, u32[]{:S(2)}) copy-start(f32[2,512,1024]{2,1,0:T(8,128)} %get-tuple-element.5) | copy-start | bytes 12582916
  138.7 2.2 %copy-start.2 = (f32[2,512,1024]{2,1,0:T(8,128)S(1)}, f32[2,512,1024]{2,1,0:T(8,128)}, u32[]{:S(2)}) copy-start(f32[2,512,1024]{2,1,0:T(8,128)} %get-tuple-element.8) | copy-start | bytes 12582916
Sparse Core Ops, SparseCore 0:
  9.9 62.8 all-gather.2
  77.5 44.9 all-gather.4
where the time goes:
time: 159 us
  waiting for transfers between devices  97.2 us (61%)
  matrix products  20.1 us (13%)
  other arithmetic  16 us (10%)
  between operations  15.5 us (10%)
  local copies, waits for them, and re-layouts  10.2 us (6%)
    all_gather x1, waiting for transfers between devices, body(): gathered = lax.all_gather(masked, 'ka', axis=0, tiled=True)  62.5 us
    all_gather x1, waiting for transfers between devices, body(): shard_part = lax.all_gather(stacked, 'pa', axis=2, tiled=True)  34.7 us
    convert_element_type x1, other arithmetic, body(): lax.dynamic_slice_in_dim(coulomb, offset, length, 2).astype(jnp.float32)  10.2 us
    dot_general x4, matrix products, body(): jnp.dot(mixed_imag, lower_half, precision=lax.Precision.HIGHEST, preferre...  8.24 us
    unnamed x10, local copies, waits for them, and re-layouts  7.4 us
    dot_general x4, matrix products, body(): jnp.dot(mixed_real, upper_half, precision=lax.Precision.HIGHEST, preferre...  6 us
  transfers between devices with their start and end apart: 2, of which 2 were waited for; matrix products, arithmetic and copies ran while one was open for 7% of the time, Pallas kernels for 0%

commit v1 on v0

v1 whole, which is shorter than its diff:
```python
import functools

import jax
import jax.numpy as jnp
from jax import lax
from jax.experimental import pallas as pl
from jax.experimental.pallas import tpu as pltpu
from jax.sharding import PartitionSpec as P

MESH = pl.DeviceIdType.MESH
PLUS, MINUS, OWN = 0, 1, 2
last_dims = (((1,), (1,)), ((), ()))
row_tile = 256


def kernel(
    ka, pa, orb, occ, plus, minus, coul, out,
    gath, first, ids_row, ids_all, ids_s, picked, cbuf, lhs,
    own_sem, coul_sem, ids_copy_sem, ids_send, ids_recv,
    first_send, first_recv, second_send, second_recv, gather_send, gather_recv,
):
    k, p = lax.axis_index("ka"), lax.axis_index("pa")
    xs = pa // 2
    z, x = p // xs, lax.rem(p, xs)
    other = 1 - z
    right, left, far = [lax.rem(x + step, xs) for step in (1, xs - 1, 2)]
    at = lambda plane, column: plane * xs + column
    half = ka // 2
    whole, low, high = pl.ds(0, ka), pl.ds(0, half), pl.ds(half, half)
    bands = out.shape[2] // 2

    own_copy = pltpu.make_async_copy(orb, gath.at[OWN, pl.ds(p, 1)], own_sem)
    own_copy.start()
    coul_copy = pltpu.make_async_copy(coul, cbuf, coul_sem)
    coul_copy.start()
    lane = lax.broadcasted_iota(jnp.int32, (1, 2 * bands), 1)
    ids_row[...] = jnp.where(lane == PLUS, plus[0], jnp.where(lane == MINUS, minus[0], occ[0]))

    barrier = pltpu.get_barrier_semaphore()

    def greet(step, carry):
        pl.semaphore_signal(barrier, inc=1, device_id=(lax.rem(k + step, ka), p), device_id_type=MESH)
        return carry

    lax.fori_loop(1, ka, greet, 0)
    for peer in (at(other, x), at(z, right), at(z, left)):
        pl.semaphore_signal(barrier, inc=1, device_id=(k, peer), device_id_type=MESH)
    own_copy.wait()
    pl.semaphore_wait(barrier, ka + 2)

    def to(source, target, send, recv, device):
        pltpu.make_async_remote_copy(
            src_ref=source, dst_ref=target, send_sem=send, recv_sem=recv,
            device_id=device, device_id_type=MESH,
        ).start()

    def arrived(ref, sem):
        pltpu.make_async_copy(ref, ref, sem).wait()

    def spread(step, carry):
        j = lax.rem(k + step, ka)
        to(ids_row, ids_all.at[k], ids_send, ids_recv, (j, p))
        to(gath.at[OWN, p, j], first.at[k], first_send, first_recv, (j, p))
        return carry

    pltpu.make_async_copy(ids_row, ids_all.at[k], ids_recv).start()
    pltpu.make_async_copy(gath.at[OWN, p, k], first.at[k], first_recv).start()
    lax.fori_loop(1, ka, spread, 0)

    def hop(item, slot, block, rows, peer):
        part = gath.at[item, block, rows]
        to(part, part, gather_send.at[item, slot], gather_recv.at[item, slot], (k, peer))

    def landed(item, slot, block, rows):
        arrived(gath.at[item, block, rows], gather_recv.at[item, slot])

    def stage_own(item):
        hop(item, 1, p, whole, at(z, right))
        hop(item, 2, p, whole, at(z, left))
        hop(item, 0, p, whole, at(other, x))

    def stage_pair(item):
        landed(item, 0, at(other, x), whole)
        hop(item, 3, at(other, x), whole, at(z, right))
        hop(item, 4, at(other, x), whole, at(z, left))

    def stage_far(item):
        landed(item, 1, at(z, left), whole)
        hop(item, 5, at(z, left), low, at(z, right))
        landed(item, 2, at(z, right), whole)
        hop(item, 6, at(z, right), high, at(z, left))

    def stage_cross(item):
        landed(item, 5, at(z, far), low)
        hop(item, 7, at(z, far), low, at(other, x))
        landed(item, 6, at(z, far), high)
        hop(item, 8, at(z, far), high, at(other, x))

    def sides(item):
        landed(item, 3, at(other, left), whole)
        landed(item, 4, at(other, right), whole)

    def last(item):
        landed(item, 7, at(other, far), low)
        landed(item, 8, at(other, far), high)

    stage_own(OWN)

    arrived(ids_all, ids_recv)
    ids_copy = pltpu.make_async_copy(ids_all, ids_s, ids_copy_sem)
    ids_copy.start()
    ids_copy.wait()
    arrived(first, first_recv)
    band = lax.rem(lax.broadcasted_iota(jnp.int32, first.shape[1:], 1), bands)

    for item in (PLUS, MINUS):
        def choose(j, carry):
            partner = ids_s[j, 0, item]
            piece = first[partner].astype(jnp.float32)
            keep = band < ids_s[partner, 0, 2]
            picked[item, j] = jnp.where(keep, piece, jnp.zeros_like(piece)).astype(jnp.bfloat16)
            return carry

        lax.fori_loop(0, ka, choose, 0)

        def deliver(step, carry):
            j = lax.rem(k + step, ka)
            to(picked.at[item, j], gath.at[item, p, k], second_send.at[item], second_recv.at[item], (j, p))
            return carry

        pltpu.make_async_copy(picked.at[item, k], gath.at[item, p, k], second_recv.at[item]).start()
        lax.fori_loop(1, ka, deliver, 0)

    stage_pair(OWN)
    stage_far(OWN)
    stage_cross(OWN)

    rows = ka * first.shape[1]
    for item in (PLUS, MINUS):
        arrived(gath.at[item, p], second_recv.at[item])
        stage_own(item)
        mine = gath[item, p].reshape(rows, 2 * bands)
        lhs[item, 0] = mine
        lhs[item, 1] = jnp.concatenate([mine[:, bands:], -mine[:, :bands]], axis=1)

    sides(OWN)
    last(OWN)
    coul_copy.wait()

    tile = min(row_tile, rows)

    def apply(block, fresh=False):
        start = pl.multiple_of(block * rows, rows)
        phi = gath[OWN, block].reshape(rows, 2 * bands)
        turned = jnp.concatenate([-phi[:, bands:], phi[:, :bands]], axis=1)
        others = [gath[item, block].reshape(rows, 2 * bands) for item in (PLUS, MINUS)]

        def one_tile(index, carry):
            here = pl.ds(pl.multiple_of(index * tile, tile), tile)
            kernels = [cbuf[item, here, pl.ds(start, rows)].astype(jnp.float32) for item in (PLUS, MINUS)]
            total = jnp.zeros((tile, 2 * bands), jnp.float32)
            for part, values in ((0, phi), (1, turned)):
                mixed = sum(
                    kernels[item]
                    * lax.dot_general(
                        lhs[item, part, here], others[item], last_dims, preferred_element_type=jnp.float32
                    )
                    for item in (PLUS, MINUS)
                )
                upper = mixed.astype(jnp.bfloat16)
                lower = (mixed - upper.astype(jnp.float32)).astype(jnp.bfloat16)
                total = total + jnp.dot(upper, values, preferred_element_type=jnp.float32)
                total = total + jnp.dot(lower, values, preferred_element_type=jnp.float32)
            if fresh:
                out[0, here] = -total
            else:
                out[0, here] = out[0, here] - total
            return carry

        lax.fori_loop(0, rows // tile, one_tile, 0)

    for item in (PLUS, MINUS):
        stage_pair(item)
    apply(p, fresh=True)
    for item in (PLUS, MINUS):
        stage_far(item)
    apply(at(other, x))
    apply(at(z, left))
    apply(at(z, right))
    for item in (PLUS, MINUS):
        stage_cross(item)
    apply(at(z, far))
    for item in (PLUS, MINUS):
        sides(item)
    apply(at(other, left))
    apply(at(other, right))
    for item in (PLUS, MINUS):
        last(item)
    apply(at(other, far))

    arrived(ids_all.at[pl.ds(0, ka - 1)], ids_send)
    arrived(first.at[pl.ds(0, ka - 1)], first_send)
    for item in (PLUS, MINUS):
        arrived(picked.at[item, pl.ds(0, ka - 1)], second_send.at[item])
    for item in (PLUS, MINUS, OWN):
        for slot in range(9):
            arrived(gath.at[item, 0, whole if slot < 5 else low], gather_send.at[item, slot])


def body(ka, pa, orbitals, occupied, plus_partner, minus_partner, coulomb):
    _, rows, channels = orbitals.shape
    piece = rows // ka
    dma = pltpu.SemaphoreType.DMA
    vmem = pl.BlockSpec(memory_space=pltpu.VMEM)
    smem = pl.BlockSpec(memory_space=pltpu.SMEM)
    hbm = pl.BlockSpec(memory_space=pl.ANY)
    return pl.pallas_call(
        functools.partial(kernel, ka, pa),
        out_shape=jax.ShapeDtypeStruct((1, rows, channels), jnp.float32),
        in_specs=[hbm, smem, smem, smem, hbm],
        out_specs=vmem,
        scratch_shapes=[
            pltpu.VMEM((3, pa, ka, piece, channels), jnp.bfloat16),
            pltpu.VMEM((ka, piece, channels), jnp.bfloat16),
            pltpu.VMEM((1, channels), jnp.int32),
            pltpu.VMEM((ka, 1, channels), jnp.int32),
            pltpu.SMEM((ka, 1, channels), jnp.int32),
            pltpu.VMEM((2, ka, piece, channels), jnp.bfloat16),
            pltpu.VMEM(coulomb.shape, jnp.bfloat16),
            pltpu.VMEM((2, 2, rows, channels), jnp.bfloat16),
            dma, dma, dma, dma, dma, dma, dma, dma((2,)), dma((2,)), dma((3, 9)), dma((3, 9)),
        ],
        compiler_params=pltpu.CompilerParams(collective_id=0, has_side_effects=True),
        name="exchange",
    )(orbitals.reshape(1, ka, piece, channels), occupied, plus_partner, minus_partner, coulomb)


def solution(mesh):
    placed = (P("ka", "pa", None), P("ka"), P("ka"), P("ka"), P(None, "pa", None))
    return jax.shard_map(
        functools.partial(body, mesh.shape["ka"], mesh.shape["pa"]),
        mesh=mesh, in_specs=placed, out_specs=P("ka", "pa", None), check_vma=False,
    )
```

time: 159 us -> 58.2 us (0.37)
  waiting for transfers between devices: 97.2 us -> 0 us
  Pallas kernels: 0 us -> 53.8 us
  matrix products: 20.1 us -> 0 us
  other arithmetic: 16 us -> 0 us
  between operations: 15.5 us -> 1.95 us
  local copies, waits for them, and re-layouts: 10.2 us -> 1.67 us
    all_gather x2 -> x0, waiting for transfers between devices: 97.2 us -> none  [the longest x1 62.5 us: body(): gathered = lax.all_gather(masked, 'ka', axis=0, tiled=True)]
    pallas_call x0 -> x1, Pallas kernels: none -> 53.8 us  [body(): pl.pallas_call(functools.partial(kernel, ka, pa), out_shape=jax.ShapeDtyp...]
    dot_general x16 -> x0, matrix products: 20.1 us -> none  [the longest x4 8.24 us: body(): jnp.dot(mixed_imag, lower_half, precision=lax.Precision.HIGHEST, preferre...]
    convert_element_type x2 -> x0, other arithmetic: 11.5 us -> none  [the longest x1 10.2 us: body(): lax.dynamic_slice_in_dim(coulomb, offset, length, 2).astype(jnp.float32)]
    unnamed x10 -> x1, local copies, waits for them, and re-layouts: 7.4 us -> 1.67 us
    gather x1 -> x0, local copies, waits for them, and re-layouts: 2.78 us -> none  [body(): jnp.take(gathered, wanted, axis=0).reshape(2, k_local, points, channels)]
    select_n x3 -> x0, other arithmetic: 1.74 us -> none  [the longest x1 1.57 us: body(): masked = jnp.where(keep_mask, orbitals, jnp.zeros_like(orbitals))]
    concatenate x1 -> x0, other arithmetic: 1.69 us -> none  [body(): stacked = jnp.concatenate([chosen, orbitals[None]], axis=0)]
  transfers between devices with their start and end apart: 2 -> 0, of which waited for: 2 -> 0; matrix products, arithmetic and copies ran while one was open for 7% -> 0% of each run, Pallas kernels for 0% -> 0%
where the time goes in v1:
time: 58.2 us; the launch traced here: 57.4 us
  Pallas kernels  53.8 us (92%)
  between operations  1.95 us (3%)
  local copies, waits for them, and re-layouts  1.67 us (3%)
    pallas_call x1, Pallas kernels, body(): pl.pallas_call(functools.partial(kernel, ka, pa), out_shape=jax.ShapeDtyp...  53.8 us
    unnamed x1, local copies, waits for them, and re-layouts  1.67 us

profile of v1, /device:TPU:8, one launch (start us, length us, event | category | flops | bytes accessed | tf_op | source)
XLA Modules:
  0.0 57.4 jit_solution(11633215678538042336)
XLA Ops:
  1.9 53.8 %exchange.1 = f32[1,512,128]{2,1,0:T(8,128)} custom-call(bf16[1,32,16,128]{3,2,1,0:T(8,128)(2,1)} %bitcast.1, s32[1]{0:T(128)S(6)} %copy.7.occ, s32[1]{0:T(128)S(6)} %copy.8.plus, s32[1]{0:T(128)S(6)} %copy.9.minus, bf16[2,512,4096]{2,1,0:T(8,128)(2,1)} %coul.1), custom_call_target="tpu_custom_call" | custom-call | tf_op jit(solution)/shard_map/exchange/pallas_call | solution.py:217
  55.7 1.7 %copy.10 = f32[1,512,128]{2,1,0:T(8,128)} copy(f32[1,512,128]{2,1,0:T(8,128)} %exchange.1) | data formatting | bytes 524288

commit v2 on v1

v2 whole, which is shorter than its diff:
```python
import functools

import jax
import jax.numpy as jnp
from jax import lax
from jax.experimental import pallas as pl
from jax.experimental.pallas import tpu as pltpu
from jax.sharding import PartitionSpec as P

MESH = pl.DeviceIdType.MESH
PLUS, MINUS, OWN = 0, 1, 2
last_dims = (((1,), (1,)), ((), ()))


def kernel(
    ka, pa, orb, occ, plus, minus, coul, out,
    gath, first, numbers, ids_row, ids_all, ids_s, picked, cbuf, lhs,
    own_sem, coul_sem, number_sems, ids_copy_sem, ids_send, ids_recv,
    first_send, first_recv, second_send, second_recv, gather_send, gather_recv,
):
    k, p = lax.axis_index("ka"), lax.axis_index("pa")
    xs = pa // 2
    z, x = p // xs, lax.rem(p, xs)
    other = 1 - z
    right, left, far = [lax.rem(x + step, xs) for step in (1, xs - 1, 2)]
    at = lambda plane, column: plane * xs + column
    half = ka // 2
    whole, low, high = (0, ka), (0, half), (half, half)
    bands = out.shape[2] // 2
    piece = first.shape[1]

    barrier = pltpu.get_barrier_semaphore()

    def greet(step, carry):
        pl.semaphore_signal(barrier, inc=1, device_id=(lax.rem(k + step, ka), p), device_id_type=MESH)
        return carry

    lax.fori_loop(1, ka, greet, 0)
    for peer in (at(other, x), at(z, right), at(z, left)):
        pl.semaphore_signal(barrier, inc=1, device_id=(k, peer), device_id_type=MESH)

    own_copy = pltpu.make_async_copy(orb, gath.at[OWN, pl.ds(p, 1)], own_sem)
    own_copy.start()
    number_copies = [
        pltpu.make_async_copy(ref, numbers.at[index], number_sems.at[index])
        for index, ref in enumerate((plus, minus, occ))
    ]
    for copy in number_copies:
        copy.start()
    coul_copy = pltpu.make_async_copy(coul, cbuf, coul_sem)
    coul_copy.start()
    for copy in number_copies:
        copy.wait()
    lane = lax.broadcasted_iota(jnp.int32, (1, 2 * bands), 1)
    ids_row[...] = jnp.where(lane == 0, numbers[0, 0], jnp.where(lane == 1, numbers[1, 0], numbers[2, 0]))
    own_copy.wait()
    pl.semaphore_wait(barrier, ka + 2)

    def to(source, target, send, recv, device):
        pltpu.make_async_remote_copy(
            src_ref=source, dst_ref=target, send_sem=send, recv_sem=recv,
            device_id=device, device_id_type=MESH,
        ).start()

    def arrived(ref, sem):
        pltpu.make_async_copy(ref, ref, sem).wait()

    def spread(step, carry):
        j = lax.rem(k + step, ka)
        to(ids_row, ids_all.at[k], ids_send, ids_recv, (j, p))
        to(gath.at[OWN, p, j], first.at[k], first_send, first_recv, (j, p))
        return carry

    pltpu.make_async_copy(ids_row, ids_all.at[k], ids_recv).start()
    pltpu.make_async_copy(gath.at[OWN, p, k], first.at[k], first_recv).start()
    lax.fori_loop(1, ka, spread, 0)

    def hop(item, slot, block, rows, peer):
        part = gath.at[item, block, pl.ds(*rows)]
        to(part, part, gather_send.at[item, slot], gather_recv.at[item, slot], (k, peer))

    def landed(item, slot, block, rows):
        arrived(gath.at[item, block, pl.ds(*rows)], gather_recv.at[item, slot])

    def send_own(item):
        hop(item, 1, p, whole, at(z, right))
        hop(item, 2, p, whole, at(z, left))
        hop(item, 0, p, whole, at(other, x))

    def send_far(item):
        landed(item, 1, at(z, left), whole)
        hop(item, 3, at(z, left), low, at(z, right))
        landed(item, 2, at(z, right), whole)
        hop(item, 4, at(z, right), high, at(z, left))

    def send_pair(item, slots, rows):
        hop(item, slots[0], at(other, x), rows, at(z, right))
        hop(item, slots[1], at(other, x), rows, at(z, left))

    def send_cross(item):
        landed(item, 3, at(z, far), low)
        hop(item, 9, at(z, far), low, at(other, x))
        landed(item, 4, at(z, far), high)
        hop(item, 10, at(z, far), high, at(other, x))

    send_own(OWN)

    arrived(ids_all, ids_recv)
    ids_copy = pltpu.make_async_copy(ids_all, ids_s, ids_copy_sem)
    ids_copy.start()
    ids_copy.wait()
    arrived(first, first_recv)
    band = lax.rem(lax.broadcasted_iota(jnp.int32, first.shape[1:], 1), bands)

    for item in (PLUS, MINUS):
        def choose(j, carry):
            partner = ids_s[j, 0, item]
            values = first[partner].astype(jnp.float32)
            keep = band < ids_s[partner, 0, 2]
            picked[item, j] = jnp.where(keep, values, jnp.zeros_like(values)).astype(jnp.bfloat16)
            return carry

        lax.fori_loop(0, ka, choose, 0)

        def deliver(step, carry):
            j = lax.rem(k + step, ka)
            to(picked.at[item, j], gath.at[item, p, k], second_send.at[item], second_recv.at[item], (j, p))
            return carry

        pltpu.make_async_copy(picked.at[item, k], gath.at[item, p, k], second_recv.at[item]).start()
        lax.fori_loop(1, ka, deliver, 0)

    send_far(OWN)
    landed(OWN, 0, at(other, x), whole)
    send_pair(OWN, (5, 7), whole)
    landed(OWN, 5, at(other, left), whole)
    hop(OWN, 9, at(other, left), low, at(z, right))
    landed(OWN, 7, at(other, right), whole)
    hop(OWN, 10, at(other, right), high, at(z, left))

    rows = ka * piece
    for item in (PLUS, MINUS):
        arrived(gath.at[item, p], second_recv.at[item])
        send_own(item)
        mine = gath[item, p].reshape(rows, 2 * bands)
        lhs[item, 0] = mine
        lhs[item, 1] = jnp.concatenate([mine[:, bands:], -mine[:, :bands]], axis=1)

    landed(OWN, 3, at(z, far), low)
    landed(OWN, 4, at(z, far), high)
    landed(OWN, 9, at(other, far), low)
    landed(OWN, 10, at(other, far), high)
    coul_copy.wait()

    def apply(block, part, fresh=False):
        pieces = pl.ds(*part)
        columns = part[1] * piece
        start = pl.multiple_of(block * rows + part[0] * piece, columns)
        phi = gath[OWN, block, pieces].reshape(columns, 2 * bands)
        turned = jnp.concatenate([-phi[:, bands:], phi[:, :bands]], axis=1)
        others = [gath[item, block, pieces].reshape(columns, 2 * bands) for item in (PLUS, MINUS)]
        kernels = [cbuf[item, :, pl.ds(start, columns)].astype(jnp.float32) for item in (PLUS, MINUS)]
        total = None
        for side, values in ((0, phi), (1, turned)):
            mixed = sum(
                kernels[item]
                * lax.dot_general(lhs[item, side], others[item], last_dims, preferred_element_type=jnp.float32)
                for item in (PLUS, MINUS)
            )
            upper = mixed.astype(jnp.bfloat16)
            lower = (mixed - upper.astype(jnp.float32)).astype(jnp.bfloat16)
            for term in (upper, lower):
                product = jnp.dot(term, values, preferred_element_type=jnp.float32)
                total = product if total is None else total + product
        out[0] = total if fresh else out[0] + total

    both = (PLUS, MINUS)
    apply(p, whole, fresh=True)
    for item in both:
        send_far(item)
        landed(item, 0, at(other, x), whole)
    for rows_part, slots in ((low, (5, 7)), (high, (6, 8))):
        for item in both:
            send_pair(item, slots, rows_part)
    apply(at(other, x), whole)
    send_cross(PLUS)
    apply(at(z, left), whole)
    send_cross(MINUS)
    apply(at(z, right), whole)
    apply(at(z, far), whole)
    for part, slots in ((low, (5, 7, 9)), (high, (6, 8, 10))):
        for block, slot in zip((at(other, left), at(other, right), at(other, far)), slots):
            for item in both:
                landed(item, slot, block, part)
            apply(block, part)

    arrived(ids_all.at[pl.ds(0, ka - 1)], ids_send)
    arrived(first.at[pl.ds(0, ka - 1)], first_send)
    for item in both:
        arrived(picked.at[item, pl.ds(0, ka - 1)], second_send.at[item])
        for slot in range(11):
            arrived(gath.at[item, 0, pl.ds(*(whole if slot < 3 else low))], gather_send.at[item, slot])
    for slot in (0, 1, 2, 3, 4, 5, 7, 9, 10):
        arrived(gath.at[OWN, 0, pl.ds(*(low if slot in (3, 4, 9, 10) else whole))], gather_send.at[OWN, slot])


def body(ka, pa, orbitals, occupied, plus_partner, minus_partner, coulomb):
    _, rows, channels = orbitals.shape
    piece = rows // ka
    dma = pltpu.SemaphoreType.DMA
    vmem = pl.BlockSpec(memory_space=pltpu.VMEM)
    hbm = pl.BlockSpec(memory_space=pl.ANY)
    summed = pl.pallas_call(
        functools.partial(kernel, ka, pa),
        out_shape=jax.ShapeDtypeStruct((1, rows, channels), jnp.float32),
        in_specs=[hbm] * 5,
        out_specs=vmem,
        scratch_shapes=[
            pltpu.VMEM((3, pa, ka, piece, channels), jnp.bfloat16),
            pltpu.VMEM((ka, piece, channels), jnp.bfloat16),
            pltpu.SMEM((3, 1), jnp.int32),
            pltpu.VMEM((1, channels), jnp.int32),
            pltpu.VMEM((ka, 1, channels), jnp.int32),
            pltpu.SMEM((ka, 1, channels), jnp.int32),
            pltpu.VMEM((2, ka, piece, channels), jnp.bfloat16),
            pltpu.VMEM(coulomb.shape, jnp.bfloat16),
            pltpu.VMEM((2, 2, rows, channels), jnp.bfloat16),
            dma, dma, dma((3,)), dma, dma, dma, dma, dma, dma((2,)), dma((2,)), dma((3, 11)), dma((3, 11)),
        ],
        compiler_params=pltpu.CompilerParams(collective_id=0, has_side_effects=True),
        name="exchange",
    )(orbitals.reshape(1, ka, piece, channels), occupied, plus_partner, minus_partner, coulomb)
    return -summed


def solution(mesh):
    placed = (P("ka", "pa", None), P("ka"), P("ka"), P("ka"), P(None, "pa", None))
    return jax.shard_map(
        functools.partial(body, mesh.shape["ka"], mesh.shape["pa"]),
        mesh=mesh, in_specs=placed, out_specs=P("ka", "pa", None), check_vma=False,
    )
```

time: 58.2 us -> 52.8 us (0.907)
  Pallas kernels: 53.8 us -> 48.5 us
  other arithmetic: 0 us -> 1.67 us
  local copies, waits for them, and re-layouts: 1.67 us -> 0 us
    pallas_call x1, Pallas kernels: 53.8 us -> 48.5 us  [body(): pl.pallas_call(functools.partial(kernel, ka, pa), out_shape=jax.ShapeDtyp...]
    neg x0 -> x1, other arithmetic: none -> 1.67 us  [body(): return -summed]
    unnamed x1 -> x0, local copies, waits for them, and re-layouts: 1.67 us -> none
where the time goes in v2:
time: 52.8 us; the launch traced here: 52.1 us
  Pallas kernels  48.5 us (92%)
  between operations  1.95 us (4%)
  other arithmetic  1.67 us (3%)
    pallas_call x1, Pallas kernels, body(): pl.pallas_call(functools.partial(kernel, ka, pa), out_shape=jax.ShapeDtyp...  48.5 us
    neg x1, other arithmetic, body(): return -summed  1.67 us

profile of v2, /device:TPU:8, one launch (start us, length us, event | category | flops | bytes accessed | tf_op | source)
XLA Modules:
  0.0 52.1 jit_solution(15686247210133742360)
XLA Ops:
  1.9 48.5 %exchange.1 = f32[1,512,128]{2,1,0:T(8,128)} custom-call(bf16[1,32,16,128]{3,2,1,0:T(8,128)(2,1)} %bitcast.1, s32[1]{0:T(128)S(6)} %copy.6.occ, s32[1]{0:T(128)S(6)} %copy.7.plus, s32[1]{0:T(128)S(6)} %copy.8.minus, bf16[2,512,4096]{2,1,0:T(8,128)(2,1)} %coul.1), custom_call_target="tpu_custom_call" | custom-call | tf_op jit(solution)/shard_map/exchange/pallas_call | solution.py:213
  50.4 1.7 %neg.3 = f32[1,512,128]{2,1,0:T(8,128)} negate(f32[1,512,128]{2,1,0:T(8,128)} %exchange.1) | non-fusion elementwise | flops 65536 | bytes 524288 | tf_op jit(solution)/shard_map/neg | solution.py:233

commit v3 on v2

--- a/solution.py
+++ b/solution.py
@@ -1,4 +1,5 @@
 import functools
+import math
 
 import jax
 import jax.numpy as jnp
@@ -9,6 +10,7 @@
 
 MESH = pl.DeviceIdType.MESH
 PLUS, MINUS, OWN = 0, 1, 2
+SPLIT = 2
 last_dims = (((1,), (1,)), ((), ()))
 
 
@@ -25,6 +27,7 @@
     right, left, far = [lax.rem(x + step, xs) for step in (1, xs - 1, 2)]
     at = lambda plane, column: plane * xs + column
     half = ka // 2
+    split = ka * SPLIT // 4
     whole, low, high = (0, ka), (0, half), (half, half)
     bands = out.shape[2] // 2
     piece = first.shape[1]
@@ -65,14 +68,18 @@
     def arrived(ref, sem):
         pltpu.make_async_copy(ref, ref, sem).wait()
 
+    def tell(step, carry):
+        to(ids_row, ids_all.at[k], ids_send, ids_recv, (lax.rem(k + step, ka), p))
+        return carry
+
     def spread(step, carry):
         j = lax.rem(k + step, ka)
-        to(ids_row, ids_all.at[k], ids_send, ids_recv, (j, p))
         to(gath.at[OWN, p, j], first.at[k], first_send, first_recv, (j, p))
         return carry
 
     pltpu.make_async_copy(ids_row, ids_all.at[k], ids_recv).start()
     pltpu.make_async_copy(gath.at[OWN, p, k], first.at[k], first_recv).start()
+    lax.fori_loop(1, ka, tell, 0)
     lax.fori_loop(1, ka, spread, 0)
 
     def hop(item, slot, block, rows, peer):
@@ -155,7 +162,7 @@
     def apply(block, part, fresh=False):
         pieces = pl.ds(*part)
         columns = part[1] * piece
-        start = pl.multiple_of(block * rows + part[0] * piece, columns)
+        start = pl.multiple_of(block * rows + part[0] * piece, math.gcd(columns, max(part[0] * piece, columns)))
         phi = gath[OWN, block, pieces].reshape(columns, 2 * bands)
         turned = jnp.concatenate([-phi[:, bands:], phi[:, :bands]], axis=1)
         others = [gath[item, block, pieces].reshape(columns, 2 * bands) for item in (PLUS, MINUS)]
@@ -175,21 +182,26 @@
         out[0] = total if fresh else out[0] + total
 
     both = (PLUS, MINUS)
+    early, late = (0, split), (split, ka - split)
     apply(p, whole, fresh=True)
-    for item in both:
-        send_far(item)
-        landed(item, 0, at(other, x), whole)
-    for rows_part, slots in ((low, (5, 7)), (high, (6, 8))):
-        for item in both:
-            send_pair(item, slots, rows_part)
+    send_far(PLUS)
+    landed(PLUS, 0, at(other, x), whole)
+    send_pair(PLUS, (5, 7), early)
+    send_far(MINUS)
+    send_pair(PLUS, (6, 8), late)
+    apply(at(z, left), whole)
+    send_cross(PLUS)
+    landed(MINUS, 0, at(other, x), whole)
+    send_pair(MINUS, (5, 7), early)
+    send_pair(MINUS, (6, 8), late)
+    apply(at(z, right), whole)
+    send_cross(MINUS)
     apply(at(other, x), whole)
-    send_cross(PLUS)
-    apply(at(z, left), whole)
-    send_cross(MINUS)
-    apply(at(z, right), whole)
     apply(at(z, far), whole)
-    for part, slots in ((low, (5, 7, 9)), (high, (6, 8, 10))):
-        for block, slot in zip((at(other, left), at(other, right), at(other, far)), slots):
+    for side, cross, slots in ((early, low, (5, 7, 9)), (late, high, (6, 8, 10))):
+        for block, slot, part in zip(
+            (at(other, left), at(other, right), at(other, far)), slots, (side, side, cross)
+        ):
             for item in both:
                 landed(item, slot, block, part)
             apply(block, part)
@@ -198,8 +210,9 @@
     arrived(first.at[pl.ds(0, ka - 1)], first_send)
     for item in both:
         arrived(picked.at[item, pl.ds(0, ka - 1)], second_send.at[item])
-        for slot in range(11):
-            arrived(gath.at[item, 0, pl.ds(*(whole if slot < 3 else low))], gather_send.at[item, slot])
+        for slots, part in (((0, 1, 2), whole), ((3, 4, 9, 10), low), ((5, 7), early), ((6, 8), late)):
+            for slot in slots:
+                arrived(gath.at[item, 0, pl.ds(*part)], gather_send.at[item, slot])
     for slot in (0, 1, 2, 3, 4, 5, 7, 9, 10):
         arrived(gath.at[OWN, 0, pl.ds(*(low if slot in (3, 4, 9, 10) else whole))], gather_send.at[OWN, slot])
 
@@ -227,7 +240,7 @@
             pltpu.VMEM((2, 2, rows, channels), jnp.bfloat16),
             dma, dma, dma((3,)), dma, dma, dma, dma, dma, dma((2,)), dma((2,)), dma((3, 11)), dma((3, 11)),
         ],
-        compiler_params=pltpu.CompilerParams(collective_id=0, has_side_effects=True),
+        compiler_params=pltpu.CompilerParams(collective_id=0, has_side_effects=True, vmem_limit_bytes=48 << 20),
         name="exchange",
     )(orbitals.reshape(1, ka, piece, channels), occupied, plus_partner, minus_partner, coulomb)
     return -summed

time: 52.8 us -> 51.4 us (0.973)
  Pallas kernels: 48.5 us -> 47.3 us
  other arithmetic: 1.67 us -> 0.72 us
  local copies, waits for them, and re-layouts: 0 us -> 0.9 us
    pallas_call x1, Pallas kernels: 48.5 us -> 47.3 us  [body(): pl.pallas_call(functools.partial(kernel, ka, pa), out_shape=jax.ShapeDtyp...]
    neg x1, other arithmetic: 1.67 us -> 0.72 us  [body(): return -summed]
    unnamed x0 -> x2, local copies, waits for them, and re-layouts: none -> 0.9 us
where the time goes in v3:
time: 51.4 us; the launch traced here: 50.9 us
  Pallas kernels  47.3 us (92%)
  between operations  1.96 us (4%)
  local copies, waits for them, and re-layouts  0.9 us (2%)
  other arithmetic  0.72 us (1%)
    pallas_call x1, Pallas kernels, body(): pl.pallas_call(functools.partial(kernel, ka, pa), out_shape=jax.ShapeDtyp...  47.3 us

profile of v3, /device:TPU:8, one launch (start us, length us, event | category | flops | bytes accessed | tf_op | source)
XLA Modules:
  0.0 50.9 jit_solution(17804734153307599178)
XLA Ops:
  1.9 0.0 copy-start
  2.0 0.9 %copy-done = bf16[1,512,128]{2,1,0:T(8,128)(2,1)S(1)} copy-done((bf16[1,512,128]{2,1,0:T(8,128)(2,1)S(1)}, bf16[1,512,128]{2,1,0:T(8,128)(2,1)}, u32[]{:S(2)}) %copy-start) | copy-done | bytes 131096
  2.8 47.3 %exchange.1 = f32[1,512,128]{2,1,0:T(8,128)S(1)} custom-call(bf16[1,32,16,128]{3,2,1,0:T(8,128)(2,1)S(1)} %bitcast.1, s32[1]{0:T(128)S(6)} %copy.6.occ, s32[1]{0:T(128)S(6)} %copy.7.plus, s32[1]{0:T(128)S(6)} %copy.8.minus, bf16[2,512,4096]{2,1,0:T(8,128)(2,1)} %coul.1), custom_call_target="tpu_custom_call" | custom-call | tf_op jit(solution)/shard_map/exchange/pallas_call | solution.py:226
  50.2 0.7 %neg.3 = f32[1,512,128]{2,1,0:T(8,128)} negate(f32[1,512,128]{2,1,0:T(8,128)S(1)} %exchange.1) | non-fusion elementwise | flops 65536 | bytes 524288 | tf_op jit(solution)/shard_map/neg | solution.py:246
Async XLA Ops:
  1.9 0.9 %copy-start = (bf16[1,512,128]{2,1,0:T(8,128)(2,1)S(1)}, bf16[1,512,128]{2,1,0:T(8,128)(2,1)}, u32[]{:S(2)}) copy-start(bf16[1,512,128]{2,1,0:T(8,128)(2,1)} %param.5) | copy-start | bytes 393220

commit v4 on v3

--- a/solution.py
+++ b/solution.py
@@ -1,5 +1,4 @@
 import functools
-import math
 
 import jax
 import jax.numpy as jnp
@@ -10,7 +9,6 @@
 
 MESH = pl.DeviceIdType.MESH
 PLUS, MINUS, OWN = 0, 1, 2
-SPLIT = 2
 last_dims = (((1,), (1,)), ((), ()))
 
 
@@ -27,7 +25,6 @@
     right, left, far = [lax.rem(x + step, xs) for step in (1, xs - 1, 2)]
     at = lambda plane, column: plane * xs + column
     half = ka // 2
-    split = ka * SPLIT // 4
     whole, low, high = (0, ka), (0, half), (half, half)
     bands = out.shape[2] // 2
     piece = first.shape[1]
@@ -89,10 +86,10 @@
     def landed(item, slot, block, rows):
         arrived(gath.at[item, block, pl.ds(*rows)], gather_recv.at[item, slot])
 
-    def send_own(item):
-        hop(item, 1, p, whole, at(z, right))
-        hop(item, 2, p, whole, at(z, left))
-        hop(item, 0, p, whole, at(other, x))
+    def send_own(item, part, slots):
+        hop(item, slots[1], p, part, at(z, right))
+        hop(item, slots[2], p, part, at(z, left))
+        hop(item, slots[0], p, part, at(other, x))
 
     def send_far(item):
         landed(item, 1, at(z, left), whole)
@@ -104,13 +101,11 @@
         hop(item, slots[0], at(other, x), rows, at(z, right))
         hop(item, slots[1], at(other, x), rows, at(z, left))
 
-    def send_cross(item):
-        landed(item, 3, at(z, far), low)
-        hop(item, 9, at(z, far), low, at(other, x))
-        landed(item, 4, at(z, far), high)
-        hop(item, 10, at(z, far), high, at(other, x))
-
-    send_own(OWN)
+    def cross(item, part, slot):
+        landed(item, slot, at(z, far), part)
+        hop(item, slot + 6, at(z, far), part, at(other, x))
+
+    send_own(OWN, whole, (0, 1, 2))
 
     arrived(ids_all, ids_recv)
     ids_copy = pltpu.make_async_copy(ids_all, ids_s, ids_copy_sem)
@@ -148,7 +143,11 @@
     rows = ka * piece
     for item in (PLUS, MINUS):
         arrived(gath.at[item, p], second_recv.at[item])
-        send_own(item)
+        if item == PLUS:
+            send_own(item, whole, (0, 1, 2))
+        else:
+            send_own(item, low, (0, 1, 2))
+            send_own(item, high, (11, 12, 13))
         mine = gath[item, p].reshape(rows, 2 * bands)
         lhs[item, 0] = mine
         lhs[item, 1] = jnp.concatenate([mine[:, bands:], -mine[:, :bands]], axis=1)
@@ -159,14 +158,27 @@
     landed(OWN, 10, at(other, far), high)
     coul_copy.wait()
 
-    def apply(block, part, fresh=False):
-        pieces = pl.ds(*part)
-        columns = part[1] * piece
-        start = pl.multiple_of(block * rows + part[0] * piece, math.gcd(columns, max(part[0] * piece, columns)))
-        phi = gath[OWN, block, pieces].reshape(columns, 2 * bands)
+    def apply(*parts, fresh=False):
+        def join(pieces, axis):
+            return pieces[0] if len(pieces) == 1 else jnp.concatenate(pieces, axis=axis)
+
+        def points(item):
+            return join(
+                [gath[item, block, pl.ds(*part)].reshape(part[1] * piece, 2 * bands) for block, part in parts], 0
+            )
+
+        def weights(item):
+            spans = []
+            for block, part in parts:
+                columns = part[1] * piece
+                start = pl.multiple_of(block * rows + part[0] * piece, columns)
+                spans.append(cbuf[item, :, pl.ds(start, columns)])
+            return join(spans, 1).astype(jnp.float32)
+
+        phi = points(OWN)
         turned = jnp.concatenate([-phi[:, bands:], phi[:, :bands]], axis=1)
-        others = [gath[item, block, pieces].reshape(columns, 2 * bands) for item in (PLUS, MINUS)]
-        kernels = [cbuf[item, :, pl.ds(start, columns)].astype(jnp.float32) for item in (PLUS, MINUS)]
+        others = [points(item) for item in (PLUS, MINUS)]
+        kernels = [weights(item) for item in (PLUS, MINUS)]
         total = None
         for side, values in ((0, phi), (1, turned)):
             mixed = sum(
@@ -182,37 +194,45 @@
         out[0] = total if fresh else out[0] + total
 
     both = (PLUS, MINUS)
-    early, late = (0, split), (split, ka - split)
-    apply(p, whole, fresh=True)
+    apply((p, whole), fresh=True)
     send_far(PLUS)
     landed(PLUS, 0, at(other, x), whole)
-    send_pair(PLUS, (5, 7), early)
-    send_far(MINUS)
-    send_pair(PLUS, (6, 8), late)
-    apply(at(z, left), whole)
-    send_cross(PLUS)
-    landed(MINUS, 0, at(other, x), whole)
-    send_pair(MINUS, (5, 7), early)
-    send_pair(MINUS, (6, 8), late)
-    apply(at(z, right), whole)
-    send_cross(MINUS)
-    apply(at(other, x), whole)
-    apply(at(z, far), whole)
-    for side, cross, slots in ((early, low, (5, 7, 9)), (late, high, (6, 8, 10))):
-        for block, slot, part in zip(
-            (at(other, left), at(other, right), at(other, far)), slots, (side, side, cross)
-        ):
-            for item in both:
-                landed(item, slot, block, part)
-            apply(block, part)
+    landed(MINUS, 1, at(z, left), low)
+    hop(MINUS, 3, at(z, left), low, at(z, right))
+    landed(MINUS, 2, at(z, right), low)
+    apply((at(z, left), low), (at(z, right), low))
+    landed(MINUS, 13, at(z, right), high)
+    hop(MINUS, 4, at(z, right), high, at(z, left))
+    send_pair(PLUS, (5, 7), low)
+    landed(MINUS, 12, at(z, left), high)
+    apply((at(z, left), high), (at(z, right), high))
+    cross(PLUS, low, 3)
+    cross(PLUS, high, 4)
+    landed(MINUS, 0, at(other, x), low)
+    send_pair(MINUS, (5, 7), low)
+    send_pair(PLUS, (6, 8), high)
+    landed(MINUS, 11, at(other, x), high)
+    send_pair(MINUS, (6, 8), high)
+    cross(MINUS, low, 3)
+    apply((at(other, x), whole))
+    cross(MINUS, high, 4)
+    apply((at(z, far), whole))
+    for part, slots in ((low, (5, 7, 9)), (high, (6, 8, 10))):
+        for item in both:
+            landed(item, slots[0], at(other, left), part)
+            landed(item, slots[1], at(other, right), part)
+        apply((at(other, left), part), (at(other, right), part))
+        for item in both:
+            landed(item, slots[2], at(other, far), part)
+        apply((at(other, far), part))
 
     arrived(ids_all.at[pl.ds(0, ka - 1)], ids_send)
     arrived(first.at[pl.ds(0, ka - 1)], first_send)
     for item in both:
         arrived(picked.at[item, pl.ds(0, ka - 1)], second_send.at[item])
-        for slots, part in (((0, 1, 2), whole), ((3, 4, 9, 10), low), ((5, 7), early), ((6, 8), late)):
-            for slot in slots:
-                arrived(gath.at[item, 0, pl.ds(*part)], gather_send.at[item, slot])
+        for slot in range(11 if item == PLUS else 14):
+            large = item == PLUS and slot < 3
+            arrived(gath.at[item, 0, pl.ds(*(whole if large else low))], gather_send.at[item, slot])
     for slot in (0, 1, 2, 3, 4, 5, 7, 9, 10):
         arrived(gath.at[OWN, 0, pl.ds(*(low if slot in (3, 4, 9, 10) else whole))], gather_send.at[OWN, slot])
 
@@ -238,7 +258,7 @@
             pltpu.VMEM((2, ka, piece, channels), jnp.bfloat16),
             pltpu.VMEM(coulomb.shape, jnp.bfloat16),
             pltpu.VMEM((2, 2, rows, channels), jnp.bfloat16),
-            dma, dma, dma((3,)), dma, dma, dma, dma, dma, dma((2,)), dma((2,)), dma((3, 11)), dma((3, 11)),
+            dma, dma, dma((3,)), dma, dma, dma, dma, dma, dma((2,)), dma((2,)), dma((3, 14)), dma((3, 14)),
         ],
         compiler_params=pltpu.CompilerParams(collective_id=0, has_side_effects=True, vmem_limit_bytes=48 << 20),
         name="exchange",

time: 51.4 us -> 50.6 us (0.984)
  Pallas kernels: 47.3 us -> 46.3 us
    pallas_call x1, Pallas kernels: 47.3 us -> 46.3 us  [body(): pl.pallas_call(functools.partial(kernel, ka, pa), out_shape=jax.ShapeDtyp...]
where the time goes in v4:
time: 50.6 us; the launch traced here: 49.9 us
  Pallas kernels  46.3 us (92%)
  between operations  1.96 us (4%)
  local copies, waits for them, and re-layouts  0.9 us (2%)
  other arithmetic  0.72 us (1%)
    pallas_call x1, Pallas kernels, body(): pl.pallas_call(functools.partial(kernel, ka, pa), out_shape=jax.ShapeDtyp...  46.3 us

profile of v4, /device:TPU:8, one launch (start us, length us, event | category | flops | bytes accessed | tf_op | source)
XLA Modules:
  0.0 49.9 jit_solution(1728870736514290015)
XLA Ops:
  1.9 0.0 copy-start
  2.0 0.9 %copy-done = bf16[1,512,128]{2,1,0:T(8,128)(2,1)S(1)} copy-done((bf16[1,512,128]{2,1,0:T(8,128)(2,1)S(1)}, bf16[1,512,128]{2,1,0:T(8,128)(2,1)}, u32[]{:S(2)}) %copy-start) | copy-done | bytes 131096
  2.8 46.3 %exchange.1 = f32[1,512,128]{2,1,0:T(8,128)S(1)} custom-call(bf16[1,32,16,128]{3,2,1,0:T(8,128)(2,1)S(1)} %bitcast.1, s32[1]{0:T(128)S(6)} %copy.6.occ, s32[1]{0:T(128)S(6)} %copy.7.plus, s32[1]{0:T(128)S(6)} %copy.8.minus, bf16[2,512,4096]{2,1,0:T(8,128)(2,1)} %coul.1), custom_call_target="tpu_custom_call" | custom-call | tf_op jit(solution)/shard_map/exchange/pallas_call | solution.py:246
  49.1 0.7 %neg.3 = f32[1,512,128]{2,1,0:T(8,128)} negate(f32[1,512,128]{2,1,0:T(8,128)S(1)} %exchange.1) | non-fusion elementwise | flops 65536 | bytes 524288 | tf_op jit(solution)/shard_map/neg | solution.py:266
Async XLA Ops:
  1.9 0.9 %copy-start = (bf16[1,512,128]{2,1,0:T(8,128)(2,1)S(1)}, bf16[1,512,128]{2,1,0:T(8,128)(2,1)}, u32[]{:S(2)}) copy-start(bf16[1,512,128]{2,1,0:T(8,128)(2,1)} %param.5) | copy-start | bytes 393220

commit v5 on v4

--- a/solution.py
+++ b/solution.py
@@ -14,7 +14,7 @@
 
 def kernel(
     ka, pa, orb, occ, plus, minus, coul, out,
-    gath, first, numbers, ids_row, ids_all, ids_s, picked, cbuf, lhs,
+    gath, first, numbers, ids_row, ids_all, ids_s, picked, cbuf, lhs, ready,
     own_sem, coul_sem, number_sems, ids_copy_sem, ids_send, ids_recv,
     first_send, first_recv, second_send, second_recv, gather_send, gather_recv,
 ):
@@ -158,7 +158,7 @@
     landed(OWN, 10, at(other, far), high)
     coul_copy.wait()
 
-    def apply(*parts, fresh=False):
+    def apply(*parts, fresh=False, prime=None, primed=None):
         def join(pieces, axis):
             return pieces[0] if len(pieces) == 1 else jnp.concatenate(pieces, axis=axis)
 
@@ -180,12 +180,20 @@
         others = [points(item) for item in (PLUS, MINUS)]
         kernels = [weights(item) for item in (PLUS, MINUS)]
         total = None
+        span = pl.ds(0, sum(part[1] for _, part in parts) * piece)
+
+        def share(item, side):
+            return kernels[item] * lax.dot_general(
+                lhs[item, side], others[item], last_dims, preferred_element_type=jnp.float32
+            )
+
+        if prime is not None:
+            for side in (0, 1):
+                ready[prime, side, :, span] = share(PLUS, side)
+            return
         for side, values in ((0, phi), (1, turned)):
-            mixed = sum(
-                kernels[item]
-                * lax.dot_general(lhs[item, side], others[item], last_dims, preferred_element_type=jnp.float32)
-                for item in (PLUS, MINUS)
-            )
+            plus_share = share(PLUS, side) if primed is None else ready[primed, side, :, span]
+            mixed = plus_share + share(MINUS, side)
             upper = mixed.astype(jnp.bfloat16)
             lower = (mixed - upper.astype(jnp.float32)).astype(jnp.bfloat16)
             for term in (upper, lower):
@@ -196,11 +204,12 @@
     both = (PLUS, MINUS)
     apply((p, whole), fresh=True)
     send_far(PLUS)
+    apply((at(z, left), low), (at(z, right), low), prime=0)
     landed(PLUS, 0, at(other, x), whole)
     landed(MINUS, 1, at(z, left), low)
     hop(MINUS, 3, at(z, left), low, at(z, right))
     landed(MINUS, 2, at(z, right), low)
-    apply((at(z, left), low), (at(z, right), low))
+    apply((at(z, left), low), (at(z, right), low), primed=0)
     landed(MINUS, 13, at(z, right), high)
     hop(MINUS, 4, at(z, right), high, at(z, left))
     send_pair(PLUS, (5, 7), low)
@@ -208,13 +217,14 @@
     apply((at(z, left), high), (at(z, right), high))
     cross(PLUS, low, 3)
     cross(PLUS, high, 4)
+    apply((at(other, x), whole), prime=0)
     landed(MINUS, 0, at(other, x), low)
     send_pair(MINUS, (5, 7), low)
     send_pair(PLUS, (6, 8), high)
     landed(MINUS, 11, at(other, x), high)
     send_pair(MINUS, (6, 8), high)
     cross(MINUS, low, 3)
-    apply((at(other, x), whole))
+    apply((at(other, x), whole), primed=0)
     cross(MINUS, high, 4)
     apply((at(z, far), whole))
     for part, slots in ((low, (5, 7, 9)), (high, (6, 8, 10))):
@@ -258,11 +268,12 @@
             pltpu.VMEM((2, ka, piece, channels), jnp.bfloat16),
             pltpu.VMEM(coulomb.shape, jnp.bfloat16),
             pltpu.VMEM((2, 2, rows, channels), jnp.bfloat16),
+            pltpu.VMEM((2, 2, rows, rows), jnp.float32),
             dma, dma, dma((3,)), dma, dma, dma, dma, dma, dma((2,)), dma((2,)), dma((3, 14)), dma((3, 14)),
         ],
         compiler_params=pltpu.CompilerParams(collective_id=0, has_side_effects=True, vmem_limit_bytes=48 << 20),
         name="exchange",
-    )(orbitals.reshape(1, ka, piece, channels), occupied, plus_partner, minus_partner, coulomb)
+    )(pltpu.with_memory_space_constraint(orbitals.reshape(1, ka, piece, channels), pltpu.HBM), occupied, plus_partner, minus_partner, coulomb)
     return -summed
 
 

time: 50.6 us -> 49.7 us (0.982); the launches traced: 49.9 us -> 49.6 us
  local copies, waits for them, and re-layouts: 0.9 us -> 0 us
  Pallas kernels: 46.3 us -> 46.9 us
    unnamed x2 -> x0, local copies, waits for them, and re-layouts: 0.9 us -> none
    pallas_call x1, Pallas kernels: 46.3 us -> 46.9 us  [body(): pl.pallas_call(functools.partial(kernel, ka, pa), out_shape=jax.ShapeDtyp...]
where the time goes in v5:
time: 49.7 us; the launch traced here: 49.6 us
  Pallas kernels  46.9 us (94%)
  between operations  1.95 us (4%)
  other arithmetic  0.72 us (1%)
    pallas_call x1, Pallas kernels, body(): pl.pallas_call(functools.partial(kernel, ka, pa), out_shape=jax.ShapeDtyp...  46.9 us

profile of v5, /device:TPU:8, one launch (start us, length us, event | category | flops | bytes accessed | tf_op | source)
XLA Modules:
  0.0 49.6 jit_solution(760941861192763641)
XLA Ops:
  1.9 46.9 %exchange.1 = f32[1,512,128]{2,1,0:T(8,128)S(1)} custom-call(bf16[1,32,16,128]{3,2,1,0:T(8,128)(2,1)} %bitcast.1, s32[1]{0:T(128)S(6)} %copy.6.occ, s32[1]{0:T(128)S(6)} %copy.7.plus, s32[1]{0:T(128)S(6)} %copy.8.minus, bf16[2,512,4096]{2,1,0:T(8,128)(2,1)} %coul.1), custom_call_target="tpu_custom_call" | custom-call | tf_op jit(solution)/shard_map/exchange/pallas_call | solution.py:256
  48.9 0.7 %neg.3 = f32[1,512,128]{2,1,0:T(8,128)} negate(f32[1,512,128]{2,1,0:T(8,128)S(1)} %exchange.1) | non-fusion elementwise | flops 65536 | bytes 524288 | tf_op jit(solution)/shard_map/neg | solution.py:277

commit v6 on v5

--- a/solution.py
+++ b/solution.py
@@ -212,8 +212,8 @@
     apply((at(z, left), low), (at(z, right), low), primed=0)
     landed(MINUS, 13, at(z, right), high)
     hop(MINUS, 4, at(z, right), high, at(z, left))
+    landed(MINUS, 12, at(z, left), high)
     send_pair(PLUS, (5, 7), low)
-    landed(MINUS, 12, at(z, left), high)
     apply((at(z, left), high), (at(z, right), high))
     cross(PLUS, low, 3)
     cross(PLUS, high, 4)

time: 49.7 us -> 49.7 us (level)
  no operation moved by 1% of the time
where the time goes in v6:
time: 49.7 us; the launch traced here: 49.6 us
  Pallas kernels  46.9 us (94%)
  between operations  1.95 us (4%)
  other arithmetic  0.72 us (1%)
    pallas_call x1, Pallas kernels, body(): pl.pallas_call(functools.partial(kernel, ka, pa), out_shape=jax.ShapeDtyp...  46.9 us

profile of v6, /device:TPU:8, one launch (start us, length us, event | category | flops | bytes accessed | tf_op | source)
XLA Modules:
  0.0 49.6 jit_solution(163834254696189991)
XLA Ops:
  1.9 46.9 %exchange.1 = f32[1,512,128]{2,1,0:T(8,128)S(1)} custom-call(bf16[1,32,16,128]{3,2,1,0:T(8,128)(2,1)} %bitcast.1, s32[1]{0:T(128)S(6)} %copy.6.occ, s32[1]{0:T(128)S(6)} %copy.7.plus, s32[1]{0:T(128)S(6)} %copy.8.minus, bf16[2,512,4096]{2,1,0:T(8,128)(2,1)} %coul.1), custom_call_target="tpu_custom_call" | custom-call | tf_op jit(solution)/shard_map/exchange/pallas_call | solution.py:256
  48.9 0.7 %neg.3 = f32[1,512,128]{2,1,0:T(8,128)} negate(f32[1,512,128]{2,1,0:T(8,128)S(1)} %exchange.1) | non-fusion elementwise | flops 65536 | bytes 524288 | tf_op jit(solution)/shard_map/neg | solution.py:277
